TPU v7x, 32 devices: a whole 2x2x4 slice. The times are simulated.
32 devices in a mesh: expert: 16 (over z, y, x), replica: 2 (over core).
Axes of the slice: x: 2, y: 2, z: 4, core: 2. Of those that a mesh axis runs over, the one named last changes fastest.
Arguments:
- grad_tokens: bfloat16 [4096, 3584], P(('expert', 'replica')), may hold values from -1.5 to 1.5
- gates: float32 [4096, 8], P(('expert', 'replica')), may hold values from 0.02 to 0.3
- expert_ids: int32 [4096, 8], P(('expert', 'replica')), may hold values from 0 to 15, all different within a row; in each aligned block of 128 rows (0 to 127, 128 to 255, ...) at most 80 rows name the same one
- hidden: bfloat16 [16, 2560, 1024], P('expert', 'replica'), may hold values from -11 to 11
- row_moment: float32 [16, 1024], P('expert', 'replica'), may hold values from 0.1 to 1
- col_moment: float32 [16, 3584], P('expert'), may hold values from 0.1 to 1
Outputs:
- update: bfloat16 [16, 1024, 3584], P('expert', 'replica')
- row_new: float32 [16, 1024], P('expert', 'replica')
- col_new: float32 [16, 3584], P('expert')
Inputs may be any that keep to these rules, and one draw needn't show every extreme that they name: `expert_ids`: in each device's block of 128 rows no expert is named more than 80 times.
All inputs are finite; a program needn't handle non-finite values.
Results may differ from a plain program's by a relative error of at most 0.014.
Values may be sent and summed in bfloat16 or wider, within the bound.
A program may use at most 128 MiB of HBM per device.

v0:
```python
import jax
import jax.numpy as jnp
from jax import lax
from jax.sharding import PartitionSpec as P

DECAY_RATE = 0.9
EPSILON = 1e-06


def body(grad_tokens, gates, expert_ids, hidden, row_moment, col_moment):
    expert_count = lax.axis_size("expert")
    replica_count = lax.axis_size("replica")
    choices_per = expert_ids.shape[1]
    model_width = grad_tokens.shape[1]
    capacity = hidden.shape[1] // expert_count
    local_hidden = hidden[0]
    share = local_hidden.shape[1] // replica_count
    hidden_total = share * replica_count
    flat_ids = expert_ids.reshape(-1)
    assigned = flat_ids.shape[0]
    onehot = (flat_ids[:, None] == jnp.arange(expert_count, dtype=jnp.int32)[None, :]).astype(
        jnp.int32
    )
    position = jnp.sum((jnp.cumsum(onehot, axis=0) - onehot) * onehot, axis=1)
    slot_of = flat_ids * capacity + position
    match = slot_of[None, :] == jnp.arange(expert_count * capacity, dtype=jnp.int32)[:, None]
    source = jnp.sum(jnp.where(match, jnp.arange(assigned, dtype=jnp.int32)[None, :], 0), axis=1)
    slot_weight = jnp.sum(jnp.where(match, gates.reshape(-1)[None, :], jnp.float32(0.0)), axis=1)
    token_rows = grad_tokens[source // choices_per]
    outgoing = (slot_weight[:, None] * token_rows.astype(jnp.float32)).astype(jnp.bfloat16)
    outgoing = outgoing.reshape(expert_count, capacity, model_width)
    arrived = lax.all_to_all(outgoing, "expert", split_axis=0, concat_axis=0, tiled=True).reshape(
        -1, model_width
    )
    gradient = lax.psum_scatter(
        lax.dot_general(
            local_hidden, arrived, (((0,), (0,)), ((), ())), preferred_element_type=jnp.float32
        ).astype(jnp.bfloat16),
        "replica",
        scatter_dimension=0,
        tiled=True,
    ).astype(jnp.float32)
    squares = gradient * gradient
    row_out = DECAY_RATE * row_moment[0] + (1.0 - DECAY_RATE) * (
        jnp.mean(squares, axis=1) + EPSILON
    )
    local_columns = jnp.sum(squares, axis=0)
    local_ratio = jnp.sum(squares / row_out[:, None], axis=0)
    column_total, ratio_total = lax.psum((local_columns, local_ratio), "replica")
    col_out = DECAY_RATE * col_moment[0] + (1.0 - DECAY_RATE) * (
        column_total / hidden_total + EPSILON
    )
    scaled = gradient / jnp.sqrt(row_out[:, None] * col_out[None, :])
    square_total = jnp.sum(ratio_total / col_out)
    spread = jnp.sqrt(square_total / (hidden_total * model_width))
    update = (scaled / jnp.maximum(1.0, spread)).astype(jnp.bfloat16)
    return (update[None], row_out[None], col_out[None])


def solution(mesh):
    placed = (
        P(("expert", "replica"), None),
        P(("expert", "replica"), None),
        P(("expert", "replica"), None),
        P("expert", "replica", None),
        P("expert", "replica"),
        P("expert", None),
    )
    return jax.shard_map(
        body,
        mesh=mesh,
        in_specs=placed,
        out_specs=(P("expert", "replica", None), P("expert", "replica"), P("expert", None)),
        check_vma=False,
    )
```

profile of v0, /device:TPU:0, one launch (start us, length us, event | category | flops | bytes accessed | tf_op | source)
XLA Modules:
  0.0 310.5 jit_solution(10157184352373405270)
XLA Ops:
  7.2 1.6 copy.18
  8.8 0.9 eq.39
  9.8 0.9 reshape.141
  10.7 0.6 fusion.13
  11.3 9.3 %reduce-window.6 = s32[16,8,128]{2,1,0:T(8,128)} reduce-window(s32[16,8,128]{2,1,0:T(8,128)} %fusion.13, s32[]{:T(128)} %constant.16.clone.1), window={size=1x1x128 pad=0_0x0_0x127_0}, to_apply=%region_0.0 | reduce-window | flops 2080768 | bytes 131076 | tf_op jit(solution)/shard_map/reduce-window
  20.6 1.6 slice.10
  22.2 1.0 copy.20
  23.3 0.9 broadcast_add_fusion
  24.2 0.6 select_reduce_fusion
  25.5 1.4 copy.22
  26.9 0.9 broadcast_in_dim.42
  28.5 8.1 %gather_fusion = bf16[1280,3584]{1,0:T(8,128)(2,1)} fusion(bf16[128,3584]{1,0:T(8,128)(2,1)S(1)} %copy-done.1, s32[2048]{0:T(1024)} %pad_clamp_fusion), kind=kCustom, calls=%fused_computation | custom fusion | bytes 18355200 | tf_op jit(solution)/shard_map/gather | solution.py:29
  36.6 10.5 %fusion = bf16[16,80,3584]{2,1,0:T(8,128)(2,1)} fusion(bf16[16,80,3584]{2,1,0:T(8,128)(2,1)} %bitcast.31, f32[16,80]{1,0:T(8,128)S(1)} %mul.92), kind=kLoop, calls=%fused_computation.2 | loop fusion | flops 13762560 | bytes 18355200 | tf_op jit(solution)/shard_map/convert_element_type | solution.py:30
  47.1 209.4 %all_to_all.5 = bf16[16,80,3584]{2,1,0:T(8,128)(2,1)S(1)} all-to-all(bf16[16,80,3584]{2,1,0:T(8,128)(2,1)} %fusion), channel_id=1, replica_groups=mesh['expert'=16,'replica'=2] {'expert'}, dimensions={0} | all-to-all | bytes 18350080 | tf_op jit(solution)/shard_map/all_to_all | solution.py:32
  256.5 11.8 %fusion.7 = bf16[1024,3584]{0,1:T(8,128)(2,1)} fusion(bf16[1280,3584]{1,0:T(8,128)(2,1)S(1)} %bitcast.32, bf16[1,1280,1024]{2,1,0:T(8,128)(2,1)S(1)} %copy-done), kind=kOutput, calls=%fused_computation.12 | convolution fusion | flops 9398910976 | bytes 19136512 | tf_op jit(solution)/shard_map/dot_general | solution.py:36
  268.3 0.7 copy-done.2
  269.1 12.0 %reduce-scatter.2.cloned.1.call-done = bf16[512,3584]{0,1:T(8,128)(2,1)} async-done(((bf16[1024,3584]{0,1:T(8,128)(2,1)}), bf16[512,3584]{0,1:T(8,128)(2,1)}) %reduce-scatter.2.cloned.1.call-update) | async-done | bytes 3670032 | tf_op jit(solution)/shard_map/reduce_scatter | solution.py:35
  281.0 2.9 fusion.3
  284.5 3.3 %fusion.2 = (f32[3584]{0:T(1024)S(1)}, f32[3584]{0:T(1024)S(1)}) fusion(bf16[512,3584]{0,1:T(8,128)(2,1)} %reduce-scatter.2.cloned.1.call-done, f32[512]{0:T(512)S(1)} %fusion.15), kind=kLoop, calls=%fused_computation.6 | loop fusion | flops 9167872 | bytes 3700736 | tf_op jit(solution)/shard_map/reduce_sum | solution.py:47
  287.8 3.6 %all-reduce = (f32[3584]{0:T(1024)S(1)}, f32[3584]{0:T(1024)S(1)}) all-reduce(f32[3584]{0:T(1024)S(1)} %get-tuple-element.13, f32[3584]{0:T(1024)S(1)} %get-tuple-element.12), channel_id=1, replica_groups=mesh['expert'=16,'replica'=2] {'replica'}, use_global_device_ids=true, to_apply=%region_10.11 | all-reduce | flops 7168 | bytes 57344 | tf_op jit(solution)/shard_map/psum | solution.py:49
  291.4 0.6 divide_reduce_fusion
  292.7 0.6 broadcast_in_dim.48
  293.3 4.4 %fusion.8 = bf16[1,512,3584]{1,2,0:T(8,128)(2,1)} fusion(bf16[512,3584]{0,1:T(8,128)(2,1)} %reduce-scatter.2.cloned.1.call-done, f32[]{:T(128)S(6)} %max_shard_map.3, f32[3584]{0:T(1024)S(1)} %get-tuple-element.17, f32[512]{0:T(512)S(1)} %fusion.15), kind=kLoop, calls=%fused_computation.16 | loop fusion | flops 9175040 | bytes 7356420 | tf_op jit(solution)/shard_map/broadcast_in_dim | solution.py:57
  297.8 5.9 %copy.23 = bf16[1,512,3584]{2,1,0:T(8,128)(2,1)} copy(bf16[1,512,3584]{1,2,0:T(8,128)(2,1)} %fusion.8) | data formatting | bytes 7340032
  (22 shorter events, 2.2 us)
Async XLA Ops:
  7.2 249.3 %copy-start = (bf16[1,1280,1024]{2,1,0:T(8,128)(2,1)S(1)}, bf16[1,1280,1024]{2,1,0:T(8,128)(2,1)}, u32[]{:S(2)}) copy-start(bf16[1,1280,1024]{2,1,0:T(8,128)(2,1)} %param.9) | copy-start | bytes 7864324
  7.2 21.4 %copy-start.1 = (bf16[128,3584]{1,0:T(8,128)(2,1)S(1)}, bf16[128,3584]{1,0:T(8,128)(2,1)}, u32[]{:S(2)}) copy-start(bf16[128,3584]{1,0:T(8,128)(2,1)} %param.6) | copy-start | bytes 2752516
  7.2 273.8 %reduce-scatter.2.cloned.1.call-start = ((), (), s32[]{:S(2)}) async-start(), calls=%async_computation.2 | async-start | bytes 11010048 | tf_op jit(solution)/shard_map/reduce_scatter | solution.py:35
  268.3 0.7 copy-start.2
  268.3 15.6 %copy-start.3 = (f32[1,512]{1,0:T(1,128)S(1)}, f32[1,512]{1,0:T(1,128)}, u32[]{:S(2)}) copy-start(f32[1,512]{1,0:T(1,128)} %param.10) | copy-start | bytes 6148
Sparse Core Ops, SparseCore 0:
  268.4 12.5 reduce-scatter.1
where the time goes:
time: 312 us; the launch traced here: 311 us
  blocking collectives  213 us (68%)
  other arithmetic  35.2 us (11%)
  local copies, waits for them, and re-layouts  23.8 us (8%)
  between operations  14.8 us (5%)
  waiting for transfers between devices  12 us (4%)
  matrix products  11.8 us (4%)
    all_to_all x1, blocking collectives, body(): lax.all_to_all(outgoing, 'expert', split_axis=0, concat_axis=0, tiled=True)  209 us
    reduce_scatter x1, waiting for transfers between devices, body(): lax.psum_scatter(lax.dot_general(local_hidden, arrived, (((0,), (0,)), ((...  12 us
    dot_general x1, matrix products, body(): lax.dot_general(local_hidden, arrived, (((0,), (0,)), ((), ())), preferre...  11.8 us
    convert_element_type x1, other arithmetic, body(): (slot_weight[:, None] * token_rows.astype(jnp.float32)).astype(jnp.bfloat16)  10.5 us
    another operation x3, other arithmetic  10.3 us
    unnamed x11, local copies, waits for them, and re-layouts  9.62 us
    gather x1, local copies, waits for them, and re-layouts, body(): token_rows = grad_tokens[source // choices_per]  8.07 us
  transfers between devices with their start and end apart: 1, of which 1 were waited for; matrix products, arithmetic and copies ran while one was open for 0% of the time, Pallas kernels for 0%

commit v1 on v0

v1 whole, which is shorter than its diff:
```python
import functools

import jax
import jax.numpy as jnp
from jax import lax
from jax.experimental import pallas as pl
from jax.experimental.pallas import tpu as pltpu
from jax.sharding import PartitionSpec as P

DECAY_RATE = 0.9
EPSILON = 1e-06
MESH = pl.DeviceIdType.MESH
LANES = 128
PAIR = 2 * LANES


def grid_of(count):
    line = 4 if count % 4 == 0 else 1
    rest, bits = count // line, []
    while rest > 1:
        if rest % 2:
            return count, []
        rest //= 2
        bits.append(rest)
    return line, bits


def chunk_plan(tiles, bits, rounds):
    forward = list(range(len(bits)))
    backward = forward[::-1]
    orders = [["line"] + backward, ["line"] + forward, backward + ["line"], forward + ["line"]]
    pairs = tiles // 2
    plan, start = [], 0
    for index in range(rounds):
        stop = 2 * (pairs * (index + 1) // rounds)
        count = stop - start
        late = max(2, round(count * 3 / 14))
        left = count - late
        sizes = [0, 0, 0, 0]
        sizes[index % 2] = left - left // 2
        sizes[1 - index % 2] = left // 2
        sizes[2 + index % 2] = late - late // 2
        sizes[3 - index % 2] = late // 2
        at = start
        pieces = []
        for order, size in zip(orders, sizes):
            if size > 0:
                pieces.append((at, size, order))
                at += size
        plan.append(pieces)
        start = stop
    return plan


def kernel(cfg, meta_hbm, tok_hbm, hid_hbm, row_ref, col_ref, upd_hbm, row_out, col_out,
           tok, meta, hid, hid_t, onehot, weight, sent, part, got, grad, row_acc, cols, cols_got,
           sem_in, sem_meta_s, sem_meta_r, sem_s, sem_r, sem_part_s, sem_part_r, sem_col_s,
           sem_col_r, sem_out):
    experts, replicas, line, bits, plan, starts, cap, share = cfg
    expert = lax.axis_index("expert")
    replica = lax.axis_index("replica")
    stride = experts // line
    place = expert // stride
    inner = expert % stride
    tiles = tok.shape[0]
    pairs = tiles // 2
    width = tiles * LANES
    hidden_total = share * replicas

    table = [sorted((q for q in range(line) if q != p), key=lambda q: (abs(q - p), q)) for p in range(line)]

    def line_source(rank):
        if rank == 0:
            return place
        value = jnp.int32(0)
        for p in range(line):
            value = value + jnp.where(place == p, jnp.int32(table[p][rank - 1]), 0)
        return value

    line_of = [line_source(rank) for rank in range(line)]

    def flipped(index, bit):
        digit = (index // bits[bit]) % 2
        return index + bits[bit] * (1 - 2 * digit)

    def source_of(rank, mask):
        where = inner
        for bit in range(len(bits)):
            if mask >> bit & 1:
                where = flipped(where, bit)
        return line_of[rank] * stride + where

    copies = []

    def load(src, dst, sem):
        copy = pltpu.make_async_copy(src, dst, sem)
        copy.start()
        return copy

    loads = []
    for tile in range(tiles):
        loads.append(load(tok_hbm.at[:, pl.ds(tile * LANES, LANES)], tok.at[tile, expert], sem_in.at[tile]))
    load_meta = load(meta_hbm, meta.at[expert], sem_in.at[tiles])
    load_hid = load(hid_hbm, hid, sem_in.at[tiles + 1])

    barrier = pltpu.get_barrier_semaphore()
    right_ok, left_ok = place + 1 < line, place > 0
    if line > 1:
        @pl.when(right_ok)
        def _():
            pl.semaphore_signal(barrier, inc=1, device_id=(expert + stride, replica), device_id_type=MESH)

        @pl.when(left_ok)
        def _():
            pl.semaphore_signal(barrier, inc=1, device_id=(expert - stride, replica), device_id_type=MESH)
    for bit in range(len(bits)):
        peer = place * stride + flipped(inner, bit)
        pl.semaphore_signal(barrier, inc=1, device_id=(peer, replica), device_id_type=MESH)
    for k in range(1, replicas):
        pl.semaphore_signal(barrier, inc=1, device_id=(expert, lax.rem(replica + k, replicas)), device_id_type=MESH)
    expected = len(bits) + replicas - 1 + jnp.where(right_ok, 1, 0) + jnp.where(left_ok, 1, 0)
    pl.semaphore_wait(barrier, expected)

    counters = {"tok": 0, "meta": 0}

    def send(piece, first, source, target, valid):
        start, size, _ = plan_flat[piece]
        pieces = [(tok.at[pl.ds(start, size), source], sem_s.at[counters["tok"]], sem_r.at[piece, source])]
        counters["tok"] += 1
        if first:
            pieces.append((meta.at[source], sem_meta_s.at[counters["meta"]], sem_meta_r.at[source]))
            counters["meta"] += 1

        def go():
            for ref, s_sem, r_sem in pieces:
                pltpu.make_async_remote_copy(ref, ref, s_sem, r_sem, device_id=(target, replica), device_id_type=MESH).start()

        def done():
            for ref, s_sem, r_sem in pieces:
                pltpu.make_async_remote_copy(ref, ref, s_sem, r_sem, device_id=(target, replica), device_id_type=MESH).wait_send()

        if valid is None:
            go()
        else:
            pl.when(valid)(go)
        copies.append((done, valid))

    plan_flat = [piece for pieces in plan for piece in pieces]

    def forward(piece, rank, mask):
        order = plan_flat[piece][2]
        source = source_of(rank, mask)
        at = -1
        for step, dim in enumerate(order):
            if (dim == "line" and rank > 0) or (dim != "line" and mask >> dim & 1):
                at = step
        for step, dim in enumerate(order):
            if dim == "line" and line > 1 and step >= at:
                if rank == 0:
                    send(piece, piece == 0, source, expert + stride, right_ok)
                    send(piece, piece == 0, source, expert - stride, left_ok)
                elif rank < line - 0:
                    up = line_of[rank] < place
                    target = jnp.where(up, expert + stride, expert - stride)
                    valid = jnp.where(up, place + 1 < line, place > 0)
                    send(piece, piece == 0, source, target, valid)
            elif dim != "line" and step > at:
                peer = place * stride + flipped(inner, dim)
                send(piece, piece == 0, source, peer, None)

    def arrive(piece, rank, mask):
        start, size, _ = plan_flat[piece]
        source = source_of(rank, mask)
        ref = tok.at[pl.ds(start, size), source]
        pltpu.make_async_remote_copy(ref, ref, sem_s.at[0], sem_r.at[piece, source], device_id=(expert, replica), device_id_type=MESH).wait_recv()
        if piece == 0:
            ref = meta.at[source]
            pltpu.make_async_remote_copy(ref, ref, sem_meta_s.at[0], sem_meta_r.at[source], device_id=(expert, replica), device_id_type=MESH).wait_recv()

    def transpose_hidden():
        block = PAIR
        for row in range(hid.shape[0] // block):
            for col in range(hid.shape[1] // block):
                hid_t[col * block:(col + 1) * block, row * block:(row + 1) * block] = jnp.transpose(
                    hid[row * block:(row + 1) * block, col * block:(col + 1) * block]
                )

    def route():
        values = meta[...]
        choices = values.shape[1] // 2
        tokens = values.shape[2]
        match = values[:, :choices, :] == expert.astype(jnp.float32)
        named = jnp.sum(jnp.where(match, 1.0, 0.0), axis=1)
        scale = jnp.sum(jnp.where(match, values[:, choices:, :], 0.0), axis=1)
        earlier = lax.broadcasted_iota(jnp.int32, (tokens, tokens), 0) < lax.broadcasted_iota(jnp.int32, (tokens, tokens), 1)
        position = jnp.dot(named.astype(jnp.bfloat16), jnp.where(earlier, 1.0, 0.0).astype(jnp.bfloat16), preferred_element_type=jnp.float32)
        slot = jnp.where(named > 0.5, position, -1.0 - 2.0 * cap)
        rows = lax.broadcasted_iota(jnp.int32, (2 * cap, tokens), 0).astype(jnp.float32)
        for pair in range(experts // 2):
            total = 0.0
            for half in range(2):
                source = 2 * pair + half
                hit = rows == slot[source:source + 1, :] + float(half * cap)
                onehot[pair, :, half * tokens:(half + 1) * tokens] = jnp.where(hit, 1.0, 0.0).astype(jnp.bfloat16)
                total = total + jnp.sum(jnp.where(hit, scale[source:source + 1, :], 0.0), axis=1, keepdims=True)
            weight[pair] = jnp.broadcast_to(total, (2 * cap, LANES))

    def compute(q):
        for pair in range(experts // 2):
            tokens = tok.shape[2]
            block = [tok[2 * q + half, 2 * pair:2 * pair + 2].reshape(2 * tokens, LANES) for half in range(2)]
            rows = jnp.dot(onehot[pair], jnp.concatenate(block, axis=1), preferred_element_type=jnp.float32)
            scale = weight[pair]
            sent[pair * 2 * cap:(pair + 1) * 2 * cap, :] = (rows * jnp.concatenate([scale, scale], axis=1)).astype(jnp.bfloat16)
        values = sent[...]
        step = min(share, 256)
        for owner in range(replicas):
            for at in range(0, share, step):
                low = owner * share + at
                part[q, owner, at:at + step, :] = jnp.dot(hid_t[low:low + step, :], values, preferred_element_type=jnp.float32).astype(jnp.bfloat16)

    def part_copy(q, k):
        peer = lax.rem(replica + k, replicas)
        return pltpu.make_async_remote_copy(part.at[q, peer], got.at[q, replica], sem_part_s.at[q, k], sem_part_r.at[q, replica], device_id=(expert, peer), device_id_type=MESH)

    def part_send(q):
        for k in range(1, replicas):
            part_copy(q, k).start()

    def columns(q):
        return pl.ds(pl.multiple_of(q * PAIR, PAIR), PAIR)

    def collect(q):
        total = part[q, replica].astype(jnp.float32)
        for k in range(1, replicas):
            peer = lax.rem(replica + k, replicas)
            pltpu.make_async_remote_copy(got.at[q, peer], got.at[q, peer], sem_part_s.at[q, k], sem_part_r.at[q, peer], device_id=(expert, peer), device_id_type=MESH).wait_recv()
            total = total + got[q, peer].astype(jnp.float32)
        grad[q] = total
        squares = total * total
        row_acc[...] = row_acc[...] + squares[:, :LANES] + squares[:, LANES:]
        cols[0:1, columns(q)] = jnp.sum(squares, axis=0, keepdims=True)

    def step(q):
        compute(q)
        pl.when(q >= 1)(lambda: part_send(q - 1))
        pl.when(q >= 3)(lambda: collect(q - 3))

    def steps(low, high):
        if high > low:
            def run(q, carry):
                step(q)
                return carry
            lax.fori_loop(low, high, run, 0)

    for copy in loads:
        copy.wait()
    load_meta.wait()
    gap = 4
    events = []
    base = 0
    for index, pieces in enumerate(plan):
        for order_at in range(len(pieces)):
            piece = base + order_at
            for rank in range(line):
                for mask in range(1 << len(bits)):
                    wave = rank + bin(mask).count("1") + gap * index
                    events.append((wave, index, rank, mask, piece))
        base += len(pieces)
    events.sort()
    remaining = [sum(1 for e in events if e[1] == index) for index in range(len(plan))]
    ends = [pieces[-1][0] + pieces[-1][1] for pieces in plan]
    ready, done_steps = 0, 0
    prepared = False
    hidden_ready = False
    events_left = len(events)
    since = 0
    for wave, index, rank, mask, piece in events:
        if rank or mask:
            arrive(piece, rank, mask)
        forward(piece, rank, mask)
        events_left -= 1
        since += 1
        remaining[index] -= 1
        if not hidden_ready and wave >= 1:
            load_hid.wait()
            transpose_hidden()
            row_acc[...] = jnp.zeros_like(row_acc)
            hidden_ready = True
        if remaining[index] == 0:
            ready = ends[index] // 2
            if not prepared:
                route()
                prepared = True
            since = 0
        elif done_steps < ready and since >= 6:
            run_to = min(ready, done_steps + 1)
            steps(done_steps, run_to)
            done_steps = run_to
            since = 0
    steps(done_steps, pairs)
    part_send(pairs - 1)
    for q in range(max(0, pairs - 3), pairs):
        collect(q)

    old_row = jnp.transpose(jnp.broadcast_to(row_ref[...], (LANES, share)))[:, :1]
    row_new = DECAY_RATE * old_row + (1.0 - DECAY_RATE) * (jnp.sum(row_acc[...], axis=1, keepdims=True) / width + EPSILON)
    row_inverse = 1.0 / row_new

    def ratio(q, carry):
        values = grad[q]
        cols[1:2, columns(q)] = jnp.sum(values * values * row_inverse, axis=0, keepdims=True)
        return carry

    lax.fori_loop(0, pairs, ratio, 0)
    row_out[...] = jnp.transpose(jnp.broadcast_to(row_new, (share, LANES)))[0:1, :]
    row_scale = 1.0 / jnp.sqrt(row_new)

    def col_copy(k):
        peer = lax.rem(replica + k, replicas)
        return pltpu.make_async_remote_copy(cols, cols_got.at[replica], sem_col_s.at[k], sem_col_r.at[replica], device_id=(expert, peer), device_id_type=MESH)

    for k in range(1, replicas):
        col_copy(k).start()
    total = cols[...]
    for done, valid in copies:
        if valid is None:
            done()
        else:
            pl.when(valid)(done)

    def drain(q, carry):
        for k in range(1, replicas):
            part_copy(q, k).wait_send()
        return carry

    lax.fori_loop(0, pairs, drain, 0)
    for k in range(1, replicas):
        peer = lax.rem(replica + k, replicas)
        pltpu.make_async_remote_copy(cols, cols_got.at[peer], sem_col_s.at[k], sem_col_r.at[peer], device_id=(expert, peer), device_id_type=MESH).wait_recv()
        total = total + cols_got[peer]
    for k in range(1, replicas):
        col_copy(k).wait_send()
    col_new = DECAY_RATE * col_ref[...] + (1.0 - DECAY_RATE) * (total[0:1] / hidden_total + EPSILON)
    col_out[...] = col_new
    spread = jnp.sqrt(jnp.sum(total[1:2] / col_new, axis=1, keepdims=True) / (hidden_total * width))
    cols[0:1, :] = 1.0 / (jnp.sqrt(col_new) * jnp.maximum(1.0, spread))

    def out_copy(q):
        return pltpu.make_async_copy(part.at[q, 0], upd_hbm.at[:, columns(q)], sem_out.at[q])

    def finish(q, carry):
        part[q, 0] = (grad[q] * row_scale * cols[0:1, columns(q)]).astype(jnp.bfloat16)
        out_copy(q).start()
        return carry

    def settle(q, carry):
        out_copy(q).wait()
        return carry

    lax.fori_loop(0, pairs, finish, 0)
    lax.fori_loop(0, pairs, settle, 0)


def body(grad_tokens, gates, expert_ids, hidden, row_moment, col_moment):
    experts = lax.axis_size("expert")
    replicas = lax.axis_size("replica")
    choices = expert_ids.shape[1]
    tokens, width = grad_tokens.shape
    slots, hidden_total = hidden.shape[1:]
    cap = slots // experts
    share = hidden_total // replicas
    line, bits = grid_of(experts)
    tiles = width // LANES
    plan = chunk_plan(tiles, bits, 2)
    pieces = sum(len(p) for p in plan)
    pairs = tiles // 2
    sends = pieces * experts * (len(bits) + 2)
    meta = jnp.concatenate([expert_ids.T.astype(jnp.float32), gates.T], axis=0)
    dma = pltpu.SemaphoreType.DMA
    vmem = pl.BlockSpec(memory_space=pltpu.VMEM)
    anywhere = pl.BlockSpec(memory_space=pl.ANY)
    cfg = (experts, replicas, line, bits, plan, None, cap, share)
    update, row_new, col_new = pl.pallas_call(
        functools.partial(kernel, cfg),
        name="routed_down_backward",
        out_shape=(
            jax.ShapeDtypeStruct((share, width), jnp.bfloat16),
            jax.ShapeDtypeStruct((1, share), jnp.float32),
            jax.ShapeDtypeStruct((1, width), jnp.float32),
        ),
        in_specs=[anywhere, anywhere, anywhere, vmem, vmem],
        out_specs=(anywhere, vmem, vmem),
        scratch_shapes=[
            pltpu.VMEM((tiles, experts, tokens, LANES), jnp.bfloat16),
            pltpu.VMEM((experts, 2 * choices, tokens), jnp.float32),
            pltpu.VMEM((slots, hidden_total), jnp.bfloat16),
            pltpu.VMEM((hidden_total, slots), jnp.bfloat16),
            pltpu.VMEM((experts // 2, 2 * cap, 2 * tokens), jnp.bfloat16),
            pltpu.VMEM((experts // 2, 2 * cap, LANES), jnp.float32),
            pltpu.VMEM((slots, PAIR), jnp.bfloat16),
            pltpu.VMEM((pairs, replicas, share, PAIR), jnp.bfloat16),
            pltpu.VMEM((pairs, replicas, share, PAIR), jnp.bfloat16),
            pltpu.VMEM((pairs, share, PAIR), jnp.float32),
            pltpu.VMEM((share, LANES), jnp.float32),
            pltpu.VMEM((2, width), jnp.float32),
            pltpu.VMEM((replicas, 2, width), jnp.float32),
            dma((tiles + 2,)),
            dma((experts * (len(bits) + 2),)),
            dma((experts,)),
            dma((sends,)),
            dma((pieces, experts)),
            dma((pairs, replicas)),
            dma((pairs, replicas)),
            dma((replicas,)),
            dma((replicas,)),
            dma((pairs,)),
        ],
        compiler_params=pltpu.CompilerParams(
            collective_id=0, has_side_effects=True, vmem_limit_bytes=62 * 1024 * 1024
        ),
    )(meta, grad_tokens, hidden[0], row_moment, col_moment)
    return (update[None], row_new, col_new)


def solution(mesh):
    placed = (
        P(("expert", "replica"), None),
        P(("expert", "replica"), None),
        P(("expert", "replica"), None),
        P("expert", "replica", None),
        P("expert", "replica"),
        P("expert", None),
    )
    return jax.shard_map(
        body,
        mesh=mesh,
        in_specs=placed,
        out_specs=(P("expert", "replica", None), P("expert", "replica"), P("expert", None)),
        check_vma=False,
    )
```

time: 312 us -> 152 us (0.49)
  blocking collectives: 213 us -> 0 us
  Pallas kernels: 0 us -> 144 us
  other arithmetic: 35.2 us -> 1.98 us
  local copies, waits for them, and re-layouts: 23.8 us -> 5.3 us
  between operations: 14.8 us -> 0.66 us
  waiting for transfers between devices: 12 us -> 0 us
  matrix products: 11.8 us -> 0 us
    all_to_all x1 -> x0, blocking collectives: 209 us -> none  [body(): lax.all_to_all(outgoing, 'expert', split_axis=0, concat_axis=0, tiled=True)]
    pallas_call x0 -> x1, Pallas kernels: none -> 144 us  [body(): pl.pallas_call(functools.partial(kernel, cfg), name='routed_down_backward...]
    reduce_scatter x1 -> x0, waiting for transfers between devices: 12 us -> none  [body(): lax.psum_scatter(lax.dot_general(local_hidden, arrived, (((0,), (0,)), ((...]
    dot_general x1 -> x0, matrix products: 11.8 us -> none  [body(): lax.dot_general(local_hidden, arrived, (((0,), (0,)), ((), ())), preferre...]
    convert_element_type x2 -> x1, other arithmetic: 11.1 us -> 0.69 us  [body(): meta = jnp.concatenate([expert_ids.T.astype(jnp.float32), gates.T], axis=0)]
    another operation x3 -> x0, other arithmetic: 10.3 us -> none
    reduce_sum x6 -> x0, other arithmetic: 8.08 us -> none  [the longest x1 3.35 us: body(): local_columns = jnp.sum(squares, axis=0)]
    gather x1 -> x0, local copies, waits for them, and re-layouts: 8.07 us -> none  [body(): token_rows = grad_tokens[source // choices_per]]
  transfers between devices with their start and end apart: 1 -> 0, of which waited for: 1 -> 0; matrix products, arithmetic and copies ran while one was open for 0% -> 0% of each run, Pallas kernels for 0% -> 0%
where the time goes in v1:
time: 152 us
  Pallas kernels  144 us (95%)
  local copies, waits for them, and re-layouts  5.3 us (3%)
  other arithmetic  1.98 us (1%)
    pallas_call x1, Pallas kernels, body(): pl.pallas_call(functools.partial(kernel, cfg), name='routed_down_backward...  144 us
    unnamed x7, local copies, waits for them, and re-layouts  5.3 us

profile of v1, /device:TPU:0, one launch (start us, length us, event | category | flops | bytes accessed | tf_op | source)
XLA Modules:
  0.0 152.0 jit_solution(18123619010501737204)
XLA Ops:
  0.6 0.7 convert_bitcast_fusion
  1.3 1.3 pad_maximum_fusion.meta_hbm
  2.6 144.1 %routed_down_backward.1 = (bf16[512,3584]{1,0:T(8,128)(2,1)}, f32[1,512]{1,0:T(1,128)}, f32[1,3584]{1,0:T(1,128)}) custom-call(f32[16,128]{1,0:T(8,128)} %pad_maximum_fusion.meta_hbm, bf16[128,3584]{1,0:T(8,128)(2,1)} %tok_hbm.1, bf16[1280,1024]{1,0:T(8,128)(2,1)} %bitcast.6, f32[1,512]{1,0:T(1,128)} %row_ref.1, f32[1,3584]{1,0:T(1,128)} %col_ref.1), custom_call_target="tpu_custom_call" | custom-call | tf_op jit(solution)/shard_map/routed_down_backward/pallas_call | solution.py:384
  146.7 0.0 copy-start.1
  146.7 0.0 copy-start
  146.7 4.1 %copy.12 = bf16[1,512,3584]{2,1,0:T(8,128)(2,1)} copy(bf16[1,512,3584]{2,1,0:T(8,128)(2,1)} %bitcast.5) | data formatting | bytes 7340032
  150.9 0.0 copy-done.1
  150.9 0.6 copy.13
  151.4 0.0 copy-done
  151.4 0.6 copy.14
Async XLA Ops:
  146.7 4.1 %copy-start.1 = (f32[1,512]{1,0:T(1,128)S(1)}, f32[1,512]{1,0:T(1,128)}, u32[]{:S(2)}) copy-start(f32[1,512]{1,0:T(1,128)} %get-tuple-element.13) | copy-start | bytes 6148
  146.7 4.7 %copy-start = (f32[1,3584]{1,0:T(1,128)S(1)}, f32[1,3584]{1,0:T(1,128)}, u32[]{:S(2)}) copy-start(f32[1,3584]{1,0:T(1,128)} %get-tuple-element.14) | copy-start | bytes 43012

commit v2 on v1

--- a/solution.py
+++ b/solution.py
@@ -12,6 +12,10 @@
 MESH = pl.DeviceIdType.MESH
 LANES = 128
 PAIR = 2 * LANES
+ROUNDS = 2
+LATE = 2 / 7
+GAP = 3
+EVERY = 2
 
 
 def grid_of(count):
@@ -28,13 +32,14 @@
 def chunk_plan(tiles, bits, rounds):
     forward = list(range(len(bits)))
     backward = forward[::-1]
-    orders = [["line"] + backward, ["line"] + forward, backward + ["line"], forward + ["line"]]
+    orders = [["line"] + backward, ["line"] + forward]
+    orders += [way[:-1] + ["line"] + way[-1:] for way in (backward, forward)]
     pairs = tiles // 2
     plan, start = [], 0
     for index in range(rounds):
         stop = 2 * (pairs * (index + 1) // rounds)
         count = stop - start
-        late = max(2, round(count * 3 / 14))
+        late = max(2, round(count * LATE))
         left = count - late
         sizes = [0, 0, 0, 0]
         sizes[index % 2] = left - left // 2
@@ -53,7 +58,7 @@
 
 
 def kernel(cfg, meta_hbm, tok_hbm, hid_hbm, row_ref, col_ref, upd_hbm, row_out, col_out,
-           tok, meta, hid, hid_t, onehot, weight, sent, part, got, grad, row_acc, cols, cols_got,
+           tok, meta, hid, hid_t, onehot, weight, earlier, sent, stage, part, got, grad, row_acc, cols, cols_got,
            sem_in, sem_meta_s, sem_meta_r, sem_s, sem_r, sem_part_s, sem_part_r, sem_col_s,
            sem_col_r, sem_out):
     experts, replicas, line, bits, plan, starts, cap, share = cfg
@@ -97,10 +102,21 @@
         copy.start()
         return copy
 
+    lasts = [bits[0], bits[-1]]
+
+    def side(piece):
+        return lasts.index(bits[plan_flat[piece][2][-1]])
+
+    def block_of(source, way):
+        low = lasts[way]
+        return (source // (2 * low)) * low + source % low
+
+    plan_flat = [piece for pieces in plan for piece in pieces]
     loads = []
-    for tile in range(tiles):
-        loads.append(load(tok_hbm.at[:, pl.ds(tile * LANES, LANES)], tok.at[tile, expert], sem_in.at[tile]))
-    load_meta = load(meta_hbm, meta.at[expert], sem_in.at[tiles])
+    for piece, (start, size, _) in enumerate(plan_flat):
+        for tile in range(start, start + size):
+            loads.append(load(tok_hbm.at[:, pl.ds(tile * LANES, LANES)], tok.at[tile, block_of(expert, side(piece))], sem_in.at[tile]))
+    load_meta = [load(meta_hbm, meta.at[way, block_of(expert, way)], sem_in.at[tiles + 2 + way]) for way in range(2)]
     load_hid = load(hid_hbm, hid, sem_in.at[tiles + 1])
 
     barrier = pltpu.get_barrier_semaphore()
@@ -122,33 +138,39 @@
     pl.semaphore_wait(barrier, expected)
 
     counters = {"tok": 0, "meta": 0}
-
-    def send(piece, first, source, target, valid):
+    pending = []
+
+    def send(parts, target, valid):
+        def each(act):
+            for src, dst, s_sem, r_sem in parts:
+                act(pltpu.make_async_remote_copy(src, dst, s_sem, r_sem, device_id=(target, replica), device_id_type=MESH))
+
+        def go():
+            each(lambda copy: copy.start())
+
+        def done():
+            each(lambda copy: copy.wait_send())
+
+        copies.append((done, valid))
+        return go if valid is None else (lambda: pl.when(valid)(go))
+
+    def next_sem():
+        counters["tok"] += 1
+        return sem_s.at[counters["tok"] - 1]
+
+    def raw_parts(piece, source):
         start, size, _ = plan_flat[piece]
-        pieces = [(tok.at[pl.ds(start, size), source], sem_s.at[counters["tok"]], sem_r.at[piece, source])]
-        counters["tok"] += 1
-        if first:
-            pieces.append((meta.at[source], sem_meta_s.at[counters["meta"]], sem_meta_r.at[source]))
+        way = side(piece)
+        ref = tok.at[pl.ds(start, size), block_of(source, way)]
+        parts = [(ref, ref, next_sem(), sem_r.at[piece, source])]
+        if piece < 2:
+            ref = meta.at[way, block_of(source, way)]
+            parts.append((ref, ref, sem_meta_s.at[way, counters["meta"]], sem_meta_r.at[way, source]))
             counters["meta"] += 1
-
-        def go():
-            for ref, s_sem, r_sem in pieces:
-                pltpu.make_async_remote_copy(ref, ref, s_sem, r_sem, device_id=(target, replica), device_id_type=MESH).start()
-
-        def done():
-            for ref, s_sem, r_sem in pieces:
-                pltpu.make_async_remote_copy(ref, ref, s_sem, r_sem, device_id=(target, replica), device_id_type=MESH).wait_send()
-
-        if valid is None:
-            go()
-        else:
-            pl.when(valid)(go)
-        copies.append((done, valid))
-
-    plan_flat = [piece for pieces in plan for piece in pieces]
+        return parts
 
     def forward(piece, rank, mask):
-        order = plan_flat[piece][2]
+        order = plan_flat[piece][2][:-1]
         source = source_of(rank, mask)
         at = -1
         for step, dim in enumerate(order):
@@ -157,25 +179,79 @@
         for step, dim in enumerate(order):
             if dim == "line" and line > 1 and step >= at:
                 if rank == 0:
-                    send(piece, piece == 0, source, expert + stride, right_ok)
-                    send(piece, piece == 0, source, expert - stride, left_ok)
-                elif rank < line - 0:
+                    send(raw_parts(piece, source), expert + stride, right_ok)()
+                    send(raw_parts(piece, source), expert - stride, left_ok)()
+                elif rank < line:
                     up = line_of[rank] < place
                     target = jnp.where(up, expert + stride, expert - stride)
-                    valid = jnp.where(up, place + 1 < line, place > 0)
-                    send(piece, piece == 0, source, target, valid)
+                    send(raw_parts(piece, source), target, jnp.where(up, place + 1 < line, place > 0))()
             elif dim != "line" and step > at:
-                peer = place * stride + flipped(inner, dim)
-                send(piece, piece == 0, source, peer, None)
+                send(raw_parts(piece, source), place * stride + flipped(inner, dim), None)()
+
+    def landed(ref, sem):
+        pltpu.make_async_remote_copy(ref, ref, sem_s.at[0], sem, device_id=(expert, replica), device_id_type=MESH).wait_recv()
+
+    def leaf(piece, mask):
+        return mask >> plan_flat[piece][2][-1] & 1
 
     def arrive(piece, rank, mask):
         start, size, _ = plan_flat[piece]
         source = source_of(rank, mask)
-        ref = tok.at[pl.ds(start, size), source]
-        pltpu.make_async_remote_copy(ref, ref, sem_s.at[0], sem_r.at[piece, source], device_id=(expert, replica), device_id_type=MESH).wait_recv()
-        if piece == 0:
-            ref = meta.at[source]
-            pltpu.make_async_remote_copy(ref, ref, sem_meta_s.at[0], sem_meta_r.at[source], device_id=(expert, replica), device_id_type=MESH).wait_recv()
+        way = side(piece)
+        if leaf(piece, mask):
+            landed(sent.at[pl.ds(start, size), source], sem_r.at[piece, source])
+            return
+        landed(tok.at[pl.ds(start, size), block_of(source, way)], sem_r.at[piece, source])
+        if piece < 2:
+            landed(meta.at[way, block_of(source, way)], sem_meta_r.at[way, source])
+
+    def peer_of(way):
+        return place * stride + flipped(inner, bits.index(lasts[way]))
+
+    def route(way, source):
+        block = block_of(source, way)
+        values = meta[way, block]
+        choices = values.shape[0] // 2
+        tokens = values.shape[1]
+        named, scale = [], []
+        for target in (expert, peer_of(way)):
+            match = values[:choices, :] == target.astype(jnp.float32)
+            named.append(jnp.sum(jnp.where(match, 1.0, 0.0), axis=0, keepdims=True))
+            scale.append(jnp.sum(jnp.where(match, values[choices:, :], 0.0), axis=0, keepdims=True))
+        both = jnp.concatenate([jnp.broadcast_to(row, (8, tokens)) for row in named], axis=0)
+        position = jnp.dot(both.astype(jnp.bfloat16), earlier[...], preferred_element_type=jnp.float32)
+        rows = lax.broadcasted_iota(jnp.int32, (cap, tokens), 0).astype(jnp.float32)
+        for half in range(2):
+            slot = jnp.where(named[half] > 0.5, position[8 * half:8 * half + 1], -1.0)
+            hit = rows == slot
+            onehot[way, block, half * cap:(half + 1) * cap, :] = jnp.where(hit, 1.0, 0.0).astype(jnp.bfloat16)
+            total = jnp.sum(jnp.where(hit, scale[half], 0.0), axis=1, keepdims=True)
+            weight[way, block, half * cap:(half + 1) * cap, :] = jnp.broadcast_to(total, (cap, LANES))
+
+    def pack(piece, rank, mask):
+        start, size, _ = plan_flat[piece]
+        way = side(piece)
+        source = source_of(rank, mask)
+        block = block_of(source, way)
+        if piece < 2:
+            route(way, source)
+        hits = onehot[way, block]
+        scale = weight[way, block]
+        for low in range(start, start + size, 2):
+            count = min(2, start + size - low)
+            columns_in = [tok[low + k, block] for k in range(count)]
+            rows = jnp.dot(hits, jnp.concatenate(columns_in, axis=1), preferred_element_type=jnp.float32)
+            for k in range(count):
+                out = (rows[:, k * LANES:(k + 1) * LANES] * scale).astype(jnp.bfloat16)
+                sent[low + k, source] = out[:cap]
+                stage[low + k, block] = out[cap:]
+        parts = [(stage.at[pl.ds(start, size), block], sent.at[pl.ds(start, size), source], next_sem(), sem_r.at[piece, source])]
+        flush()
+        pending.append(send(parts, peer_of(way), None))
+
+    def flush():
+        while pending:
+            pending.pop()()
 
     def transpose_hidden():
         block = PAIR
@@ -185,34 +261,8 @@
                     hid[row * block:(row + 1) * block, col * block:(col + 1) * block]
                 )
 
-    def route():
-        values = meta[...]
-        choices = values.shape[1] // 2
-        tokens = values.shape[2]
-        match = values[:, :choices, :] == expert.astype(jnp.float32)
-        named = jnp.sum(jnp.where(match, 1.0, 0.0), axis=1)
-        scale = jnp.sum(jnp.where(match, values[:, choices:, :], 0.0), axis=1)
-        earlier = lax.broadcasted_iota(jnp.int32, (tokens, tokens), 0) < lax.broadcasted_iota(jnp.int32, (tokens, tokens), 1)
-        position = jnp.dot(named.astype(jnp.bfloat16), jnp.where(earlier, 1.0, 0.0).astype(jnp.bfloat16), preferred_element_type=jnp.float32)
-        slot = jnp.where(named > 0.5, position, -1.0 - 2.0 * cap)
-        rows = lax.broadcasted_iota(jnp.int32, (2 * cap, tokens), 0).astype(jnp.float32)
-        for pair in range(experts // 2):
-            total = 0.0
-            for half in range(2):
-                source = 2 * pair + half
-                hit = rows == slot[source:source + 1, :] + float(half * cap)
-                onehot[pair, :, half * tokens:(half + 1) * tokens] = jnp.where(hit, 1.0, 0.0).astype(jnp.bfloat16)
-                total = total + jnp.sum(jnp.where(hit, scale[source:source + 1, :], 0.0), axis=1, keepdims=True)
-            weight[pair] = jnp.broadcast_to(total, (2 * cap, LANES))
-
     def compute(q):
-        for pair in range(experts // 2):
-            tokens = tok.shape[2]
-            block = [tok[2 * q + half, 2 * pair:2 * pair + 2].reshape(2 * tokens, LANES) for half in range(2)]
-            rows = jnp.dot(onehot[pair], jnp.concatenate(block, axis=1), preferred_element_type=jnp.float32)
-            scale = weight[pair]
-            sent[pair * 2 * cap:(pair + 1) * 2 * cap, :] = (rows * jnp.concatenate([scale, scale], axis=1)).astype(jnp.bfloat16)
-        values = sent[...]
+        values = jnp.concatenate([sent[2 * q + k].reshape(experts * cap, LANES) for k in range(2)], axis=1)
         step = min(share, 256)
         for owner in range(replicas):
             for at in range(0, share, step):
@@ -253,10 +303,12 @@
                 return carry
             lax.fori_loop(low, high, run, 0)
 
-    for copy in loads:
+    tokens = meta.shape[3]
+    before = lax.broadcasted_iota(jnp.int32, (tokens, tokens), 0) < lax.broadcasted_iota(jnp.int32, (tokens, tokens), 1)
+    earlier[...] = jnp.where(before, 1.0, 0.0).astype(jnp.bfloat16)
+    for copy in load_meta + loads:
         copy.wait()
-    load_meta.wait()
-    gap = 4
+    gap = GAP
     events = []
     base = 0
     for index, pieces in enumerate(plan):
@@ -265,23 +317,26 @@
             for rank in range(line):
                 for mask in range(1 << len(bits)):
                     wave = rank + bin(mask).count("1") + gap * index
+                    if leaf(piece, mask):
+                        wave = line + len(bits) + gap * index
                     events.append((wave, index, rank, mask, piece))
         base += len(pieces)
     events.sort()
     remaining = [sum(1 for e in events if e[1] == index) for index in range(len(plan))]
     ends = [pieces[-1][0] + pieces[-1][1] for pieces in plan]
-    ready, done_steps = 0, 0
-    prepared = False
-    hidden_ready = False
-    events_left = len(events)
-    since = 0
+    ready, done_steps, since, hidden_ready = 0, 0, 0, False
+    raw_left = sum(1 for e in events if not leaf(e[4], e[3]))
     for wave, index, rank, mask, piece in events:
         if rank or mask:
             arrive(piece, rank, mask)
-        forward(piece, rank, mask)
-        events_left -= 1
-        since += 1
         remaining[index] -= 1
+        if not leaf(piece, mask):
+            forward(piece, rank, mask)
+            pack(piece, rank, mask)
+            since += 1
+            raw_left -= 1
+            if raw_left == 0:
+                flush()
         if not hidden_ready and wave >= 1:
             load_hid.wait()
             transpose_hidden()
@@ -289,14 +344,10 @@
             hidden_ready = True
         if remaining[index] == 0:
             ready = ends[index] // 2
-            if not prepared:
-                route()
-                prepared = True
-            since = 0
-        elif done_steps < ready and since >= 6:
-            run_to = min(ready, done_steps + 1)
-            steps(done_steps, run_to)
-            done_steps = run_to
+            since = EVERY
+        if done_steps < ready and since >= EVERY and index + 1 < len(plan) + (remaining[-1] > 0):
+            steps(done_steps, done_steps + 1)
+            done_steps += 1
             since = 0
     steps(done_steps, pairs)
     part_send(pairs - 1)
@@ -369,10 +420,17 @@
     tokens, width = grad_tokens.shape
     slots, hidden_total = hidden.shape[1:]
     cap = slots // experts
+    local_hidden = hidden[0]
+    if cap % 16:
+        padded = cap + 16 - cap % 16
+        local_hidden = jnp.pad(
+            local_hidden.reshape(experts, cap, hidden_total), ((0, 0), (0, padded - cap), (0, 0))
+        ).reshape(experts * padded, hidden_total)
+        cap, slots = padded, experts * padded
     share = hidden_total // replicas
     line, bits = grid_of(experts)
     tiles = width // LANES
-    plan = chunk_plan(tiles, bits, 2)
+    plan = chunk_plan(tiles, bits, ROUNDS)
     pieces = sum(len(p) for p in plan)
     pairs = tiles // 2
     sends = pieces * experts * (len(bits) + 2)
@@ -392,22 +450,24 @@
         in_specs=[anywhere, anywhere, anywhere, vmem, vmem],
         out_specs=(anywhere, vmem, vmem),
         scratch_shapes=[
-            pltpu.VMEM((tiles, experts, tokens, LANES), jnp.bfloat16),
-            pltpu.VMEM((experts, 2 * choices, tokens), jnp.float32),
+            pltpu.VMEM((tiles, experts // 2, tokens, LANES), jnp.bfloat16),
+            pltpu.VMEM((2, experts // 2, 2 * choices, tokens), jnp.float32),
             pltpu.VMEM((slots, hidden_total), jnp.bfloat16),
             pltpu.VMEM((hidden_total, slots), jnp.bfloat16),
-            pltpu.VMEM((experts // 2, 2 * cap, 2 * tokens), jnp.bfloat16),
-            pltpu.VMEM((experts // 2, 2 * cap, LANES), jnp.float32),
-            pltpu.VMEM((slots, PAIR), jnp.bfloat16),
+            pltpu.VMEM((2, experts // 2, 2 * cap, tokens), jnp.bfloat16),
+            pltpu.VMEM((2, experts // 2, 2 * cap, LANES), jnp.float32),
+            pltpu.VMEM((tokens, tokens), jnp.bfloat16),
+            pltpu.VMEM((tiles, experts, cap, LANES), jnp.bfloat16),
+            pltpu.VMEM((tiles, experts // 2, cap, LANES), jnp.bfloat16),
             pltpu.VMEM((pairs, replicas, share, PAIR), jnp.bfloat16),
             pltpu.VMEM((pairs, replicas, share, PAIR), jnp.bfloat16),
             pltpu.VMEM((pairs, share, PAIR), jnp.float32),
             pltpu.VMEM((share, LANES), jnp.float32),
             pltpu.VMEM((2, width), jnp.float32),
             pltpu.VMEM((replicas, 2, width), jnp.float32),
-            dma((tiles + 2,)),
-            dma((experts * (len(bits) + 2),)),
-            dma((experts,)),
+            dma((tiles + 4,)),
+            dma((2, 2 * experts * (len(bits) + 2))),
+            dma((2, experts)),
             dma((sends,)),
             dma((pieces, experts)),
             dma((pairs, replicas)),
@@ -419,7 +479,7 @@
         compiler_params=pltpu.CompilerParams(
             collective_id=0, has_side_effects=True, vmem_limit_bytes=62 * 1024 * 1024
         ),
-    )(meta, grad_tokens, hidden[0], row_moment, col_moment)
+    )(meta, grad_tokens, local_hidden, row_moment, col_moment)
     return (update[None], row_new, col_new)
 
 

time: 152 us -> 129 us (0.85)
  Pallas kernels: 144 us -> 120 us
    pallas_call x1, Pallas kernels: 144 us -> 120 us  [body(): pl.pallas_call(functools.partial(kernel, cfg), name='routed_down_backward...]
where the time goes in v2:
time: 129 us; the launch traced here: 128 us
  Pallas kernels  120 us (93%)
  local copies, waits for them, and re-layouts  5.3 us (4%)
  other arithmetic  1.98 us (2%)
    pallas_call x1, Pallas kernels, body(): pl.pallas_call(functools.partial(kernel, cfg), name='routed_down_backward...  120 us
    unnamed x7, local copies, waits for them, and re-layouts  5.3 us

profile of v2, /device:TPU:0, one launch (start us, length us, event | category | flops | bytes accessed | tf_op | source)
XLA Modules:
  0.0 128.3 jit_solution(17081279150054624777)
XLA Ops:
  0.6 0.7 convert_bitcast_fusion
  1.3 1.3 %pad_maximum_fusion.meta_hbm = f32[16,128]{1,0:T(8,128)} fusion(f32[8,128]{1,0:T(8,128)} %bitcast.7, f32[8,128]{1,0:T(8,128)S(1)} %convert_bitcast_fusion), kind=kLoop, calls=%fused_computation | loop fusion | flops 2048 | bytes 16384 | tf_op jit(solution)/shard_map/concatenate | solution.py:437
  2.6 120.3 %routed_down_backward.1 = (bf16[512,3584]{1,0:T(8,128)(2,1)}, f32[1,512]{1,0:T(1,128)}, f32[1,3584]{1,0:T(1,128)}) custom-call(f32[16,128]{1,0:T(8,128)} %pad_maximum_fusion.meta_hbm, bf16[128,3584]{1,0:T(8,128)(2,1)} %tok_hbm.1, bf16[1280,1024]{1,0:T(8,128)(2,1)} %bitcast.6, f32[1,512]{1,0:T(1,128)} %row_ref.1, f32[1,3584]{1,0:T(1,128)} %col_ref.1), custom_call_target="tpu_custom_call" | custom-call | tf_op jit(solution)/shard_map/routed_down_backward/pallas_call | solution.py:442
  123.0 0.0 copy-start.1
  123.0 0.0 copy-start
  123.0 4.1 %copy.12 = bf16[1,512,3584]{2,1,0:T(8,128)(2,1)} copy(bf16[1,512,3584]{2,1,0:T(8,128)(2,1)} %bitcast.5) | data formatting | bytes 7340032
  127.1 0.0 copy-done.1
  127.1 0.6 copy.13
  127.7 0.0 copy-done
  127.7 0.6 copy.14
Async XLA Ops:
  123.0 4.1 %copy-start.1 = (f32[1,512]{1,0:T(1,128)S(1)}, f32[1,512]{1,0:T(1,128)}, u32[]{:S(2)}) copy-start(f32[1,512]{1,0:T(1,128)} %get-tuple-element.13) | copy-start | bytes 6148
  123.0 4.7 %copy-start = (f32[1,3584]{1,0:T(1,128)S(1)}, f32[1,3584]{1,0:T(1,128)}, u32[]{:S(2)}) copy-start(f32[1,3584]{1,0:T(1,128)} %get-tuple-element.14) | copy-start | bytes 43012

commit v3 on v2

--- a/solution.py
+++ b/solution.py
@@ -37,7 +37,7 @@
     pairs = tiles // 2
     plan, start = [], 0
     for index in range(rounds):
-        stop = 2 * (pairs * (index + 1) // rounds)
+        stop = tiles if index + 1 == rounds else 2 * (pairs * (index + 1) * 9 // (rounds * 7))
         count = stop - start
         late = max(2, round(count * LATE))
         left = count - late

time: 129 us -> 131 us (1.016)
  Pallas kernels: 120 us -> 123 us
    pallas_call x1, Pallas kernels: 120 us -> 123 us  [body(): pl.pallas_call(functools.partial(kernel, cfg), name='routed_down_backward...]
where the time goes in v3:
time: 131 us
  Pallas kernels  123 us (94%)
  local copies, waits for them, and re-layouts  5.3 us (4%)
  other arithmetic  1.98 us (2%)
    pallas_call x1, Pallas kernels, body(): pl.pallas_call(functools.partial(kernel, cfg), name='routed_down_backward...  123 us
    unnamed x7, local copies, waits for them, and re-layouts  5.3 us

profile of v3, /device:TPU:0, one launch (start us, length us, event | category | flops | bytes accessed | tf_op | source)
XLA Modules:
  0.0 130.8 jit_solution(6020582564262639824)
XLA Ops:
  0.6 0.7 convert_bitcast_fusion
  1.3 1.3 pad_maximum_fusion.meta_hbm
  2.6 122.9 %routed_down_backward.1 = (bf16[512,3584]{1,0:T(8,128)(2,1)}, f32[1,512]{1,0:T(1,128)}, f32[1,3584]{1,0:T(1,128)}) custom-call(f32[16,128]{1,0:T(8,128)} %pad_maximum_fusion.meta_hbm, bf16[128,3584]{1,0:T(8,128)(2,1)} %tok_hbm.1, bf16[1280,1024]{1,0:T(8,128)(2,1)} %bitcast.6, f32[1,512]{1,0:T(1,128)} %row_ref.1, f32[1,3584]{1,0:T(1,128)} %col_ref.1), custom_call_target="tpu_custom_call" | custom-call | tf_op jit(solution)/shard_map/routed_down_backward/pallas_call | solution.py:442
  125.5 0.0 copy-start.1
  125.5 0.0 copy-start
  125.5 4.1 %copy.12 = bf16[1,512,3584]{2,1,0:T(8,128)(2,1)} copy(bf16[1,512,3584]{2,1,0:T(8,128)(2,1)} %bitcast.5) | data formatting | bytes 7340032
  129.7 0.0 copy-done.1
  129.7 0.6 copy.13
  130.2 0.0 copy-done
  130.2 0.6 copy.14
Async XLA Ops:
  125.5 4.1 %copy-start.1 = (f32[1,512]{1,0:T(1,128)S(1)}, f32[1,512]{1,0:T(1,128)}, u32[]{:S(2)}) copy-start(f32[1,512]{1,0:T(1,128)} %get-tuple-element.13) | copy-start | bytes 6148
  125.5 4.7 %copy-start = (f32[1,3584]{1,0:T(1,128)S(1)}, f32[1,3584]{1,0:T(1,128)}, u32[]{:S(2)}) copy-start(f32[1,3584]{1,0:T(1,128)} %get-tuple-element.14) | copy-start | bytes 43012
